TPU v7x, 512 devices: a whole 4x4x16 slice. The times are simulated.
512 devices in a mesh: dp: 64 (over z_hi, y, x, core), tensor: 8 (over z_lo).
Axes of the slice: x: 4, y: 4, z: 16 (z_hi: 2, z_lo: 8; z = z_hi * 8 + z_lo), core: 2. Of those that a mesh axis runs over, the one named last changes fastest.
Arguments:
- hidden: bfloat16 [8192, 7168], P('dp'), may hold values from -6 to 6
- norm_gain: bfloat16 [7168], replicated, may hold values from 0.099609375 to 1.8984375
- learner_probe_proj: float32 [7168, 4096], P(('dp', 'tensor')), may hold values from -1 to 1
- learner_lookup_proj: float32 [7168, 1024], P(('dp', 'tensor')), may hold values from -3 to 3
- learner_content_proj: float32 [7168, 1024], P(('dp', 'tensor')), may hold values from -0.0625 to 0.0625
- lengths: int32 [4], replicated, may hold values from 1 to 4096, 8192 in all
Outputs:
- serving_combined: bfloat16 [7168, 6144], P('dp', 'tensor')
- spun_lookup_vectors: bfloat16 [8192, 1024], P('dp', 'tensor')
- content_vectors: bfloat16 [8192, 1024], P('dp', 'tensor')
- attention_mix: bfloat16 [8192, 4096], P('dp', 'tensor')
Inputs may be any that keep to these rules, and one draw needn't show every extreme that they name: `lengths`: 4 prompts that fill all 8192 tokens; the longest has exactly 4096 tokens.
All inputs are finite; a program needn't handle non-finite values.
Results may differ from a plain program's by a relative error of at most 0.006.
The roundings to bfloat16 on the way count: a program that leaves them out, or rounds other values in their place, can miss the bound.
Values may be sent and summed in bfloat16 or wider, within the bound.
A program may use at most 64 MiB of HBM per device.

v0:
```python
import math
import jax
import jax.numpy as jnp
from jax import lax
from jax.sharding import PartitionSpec as P

SHARED_KV_NUM = 8
QUARTET_SHARE = 4
PER_ATTN_DIM = 128
rope_theta = 5000000.0
norm_eps = 1e-05
masked_score = -1e30


def document_start(lengths, positions):
    ends = jnp.cumsum(lengths)
    starts = ends - lengths
    inside = (positions[:, None] >= starts[None, :]) & (positions[:, None] < ends[None, :])
    return jnp.sum(jnp.where(inside, starts[None, :], 0), axis=1)


def spin_pairs(content_entries, shift_amounts):
    half_dim = content_entries.shape[-1] // 2
    inverse = rope_theta ** (
        -2.0 * jnp.arange(half_dim, dtype=jnp.float32) / content_entries.shape[-1]
    )
    angles = shift_amounts.astype(jnp.float32)[:, None] * inverse[None, :]
    cosine = jnp.cos(angles)[:, None, :]
    sine = jnp.sin(angles)[:, None, :]
    first = content_entries[..., :half_dim]
    second = content_entries[..., half_dim:]
    return jnp.concatenate(
        [first * cosine - second * sine, second * cosine + first * sine], axis=-1
    )


def per_device(
    hidden, norm_gain, learner_probe_proj, learner_lookup_proj, learner_content_proj, lengths
):
    tok_rows = hidden.shape[0]
    learner_lines = learner_probe_proj.shape[0]
    combined_slab = jnp.concatenate(
        [
            learner_probe_proj.reshape(learner_lines, SHARED_KV_NUM, QUARTET_SHARE * PER_ATTN_DIM),
            learner_lookup_proj.reshape(learner_lines, SHARED_KV_NUM, PER_ATTN_DIM),
            learner_content_proj.reshape(learner_lines, SHARED_KV_NUM, PER_ATTN_DIM),
        ],
        axis=2,
    )
    combined_slab = combined_slab.reshape(
        learner_lines, SHARED_KV_NUM * (QUARTET_SHARE + 2) * PER_ATTN_DIM
    ).astype(jnp.bfloat16)
    serving_combined = lax.all_to_all(
        combined_slab, "tensor", split_axis=1, concat_axis=0, tiled=True
    )
    local_groups = serving_combined.shape[1] // ((QUARTET_SHARE + 2) * PER_ATTN_DIM)
    widened = hidden.astype(jnp.float32)
    scale = lax.rsqrt(jnp.mean(widened * widened, axis=1, keepdims=True) + norm_eps)
    normed = (widened * scale * norm_gain.astype(jnp.float32)[None, :]).astype(jnp.bfloat16)
    mapped_result = jnp.dot(
        normed,
        lax.all_gather(serving_combined, "dp", axis=0, tiled=True),
        preferred_element_type=jnp.float32,
    )
    mapped_result = mapped_result.reshape(tok_rows, local_groups, QUARTET_SHARE + 2, PER_ATTN_DIM)
    query_part = mapped_result[:, :, :QUARTET_SHARE, :]
    key_part = mapped_result[:, :, QUARTET_SHARE, :]
    value_part = mapped_result[:, :, QUARTET_SHARE + 1, :]
    my_index = lax.axis_index("dp") * tok_rows + jnp.arange(tok_rows, dtype=jnp.int32)
    my_start = document_start(lengths, my_index)
    shift_amounts = my_index - my_start
    query_rot = spin_pairs(
        query_part.reshape(tok_rows, local_groups * QUARTET_SHARE, PER_ATTN_DIM), shift_amounts
    ).astype(jnp.bfloat16)
    spun_lookup_vectors = (
        spin_pairs(key_part, shift_amounts)
        .astype(jnp.bfloat16)
        .reshape(tok_rows, local_groups * PER_ATTN_DIM)
    )
    content_vectors = value_part.astype(jnp.bfloat16).reshape(tok_rows, local_groups * PER_ATTN_DIM)
    probe_vectors = query_rot.reshape(
        tok_rows, local_groups, QUARTET_SHARE, PER_ATTN_DIM
    ).transpose(1, 2, 0, 3)
    inv_root = 1.0 / math.sqrt(PER_ATTN_DIM)
    initial = (
        jnp.full((local_groups, QUARTET_SHARE, tok_rows, 1), masked_score, jnp.float32),
        jnp.zeros((local_groups, QUARTET_SHARE, tok_rows, 1), jnp.float32),
        jnp.zeros((local_groups, QUARTET_SHARE, tok_rows, PER_ATTN_DIM), jnp.float32),
    )
    key_piece = lax.all_gather(spun_lookup_vectors, "dp", axis=0, tiled=True)
    value_piece = lax.all_gather(content_vectors, "dp", axis=0, tiled=True)
    span = key_piece.shape[0]
    step_size = math.gcd(span, 512)

    def one_step(turn, state):
        top, total, accum = state
        begin = turn * step_size
        keys_three = lax.dynamic_slice_in_dim(key_piece, begin, step_size, 0).reshape(
            step_size, local_groups, PER_ATTN_DIM
        )
        values_three = lax.dynamic_slice_in_dim(value_piece, begin, step_size, 0).reshape(
            step_size, local_groups, PER_ATTN_DIM
        )
        key_index = begin + jnp.arange(step_size, dtype=jnp.int32)
        key_start = document_start(lengths, key_index)
        allowed = (
            (key_start[None, :] == my_start[:, None])
            & (key_index[None, :] <= my_index[:, None])
            & (key_index[None, :] >= 0)
        )
        scores = (
            jnp.einsum(
                "ghqd,kgd->ghqk", probe_vectors, keys_three, preferred_element_type=jnp.float32
            )
            * inv_root
        )
        scores = jnp.where(allowed, scores, masked_score)
        new_top = jnp.maximum(top, jnp.max(scores, axis=3, keepdims=True))
        weights = jnp.where(allowed, jnp.exp(scores - new_top), 0.0)
        fade = jnp.exp(top - new_top)
        total = total * fade + jnp.sum(weights, axis=3, keepdims=True)
        accum = accum * fade + jnp.einsum(
            "ghqk,kgd->ghqd",
            weights.astype(jnp.bfloat16),
            values_three,
            preferred_element_type=jnp.float32,
        )
        return (new_top, total, accum)

    top, total, accum = lax.fori_loop(0, span // step_size, one_step, initial)
    attention_mix = (
        (accum / total)
        .transpose(2, 0, 1, 3)
        .reshape(tok_rows, local_groups * QUARTET_SHARE * PER_ATTN_DIM)
        .astype(jnp.bfloat16)
    )
    return (serving_combined, spun_lookup_vectors, content_vectors, attention_mix)


def solution(mesh):
    in_specs = (
        P("dp", None),
        P(),
        P(("dp", "tensor"), None),
        P(("dp", "tensor"), None),
        P(("dp", "tensor"), None),
        P(),
    )
    out_specs = (P("dp", "tensor"), P("dp", "tensor"), P("dp", "tensor"), P("dp", "tensor"))
    return jax.shard_map(
        per_device, mesh=mesh, in_specs=in_specs, out_specs=out_specs, check_vma=False
    )
```

profile of v0, /device:TPU:1, one launch (start us, length us, event | category | flops | bytes accessed | tf_op | source)
XLA Modules:
  0.0 520.1 jit_solution(11853927913297743682)
XLA Ops:
  7.2 1.0 convert.33
  8.3 0.8 convert.32
  9.1 1.0 convert.31
  10.2 24.0 %all_to_all.16 = bf16[14,8,768]{2,0,1:T(8,128)(2,1)S(1)} all-to-all(bf16[14,8,768]{2,0,1:T(8,128)(2,1)S(1)} %pad_maximum_fusion), channel_id=1, replica_groups=mesh['dp'=64,'tensor'=8] {'tensor'}, dimensions={1} | all-to-all | bytes 344064 | tf_op jit(solution)/shard_map/all_to_all | solution.py:53
  34.2 0.7 all_to_all.14
  35.4 0.4 fusion.20
  35.8 195.2 %all-gather.5.cloned.1.call-done = bf16[7168,768]{1,0:T(8,128)(2,1)} async-done(((bf16[112,768]{1,0:T(8,128)(2,1)}), bf16[7168,768]{1,0:T(8,128)(2,1)}) %all-gather.5.cloned.1.call-update) | async-done | bytes 11010064 | tf_op jit(solution)/shard_map/all_gather | solution.py:62
  231.1 7.2 %fusion.23 = f32[128,768]{0,1:T(8,128)S(1)} fusion(bf16[7168,768]{1,0:T(8,128)(2,1)} %all-gather.5.cloned.1.call-done, bf16[128,7168]{1,0:T(8,128)(2,1)S(1)} %copy-done, f32[7168]{0:T(1024)S(1)} %convert_element_type.58, f32[128]{0:T(128)S(1)} %add_rsqrt_fusion), kind=kOutput, calls=%fused_computation.36 | convolution fusion | flops 1412956160 | bytes 13267456 | tf_op jit(solution)/shard_map/dot_general | solution.py:60
  238.5 0.6 pad_maximum_fusion.1
  239.2 0.6 slice.66
  240.1 1.5 copy.38
  241.6 0.7 copy.39
  242.5 105.7 %all-gather.7.cloned.1.call-done = bf16[8192,128]{0,1:T(8,128)(2,1)} async-done(((bf16[128,128]{0,1:T(8,128)(2,1)}), bf16[8192,128]{0,1:T(8,128)(2,1)}) %all-gather.7.cloned.1.call-update) | async-done | bytes 2097168 | tf_op jit(solution)/shard_map/all_gather | solution.py:90
  348.2 112.0 %all-gather.9.cloned.1.call-done = bf16[8192,1,1,128]{0,3,2,1:T(8,128)(2,1)} async-done(((bf16[128,1,1,128]{0,3,2,1:T(8,128)(2,1)}), bf16[8192,1,1,128]{0,3,2,1:T(8,128)(2,1)}) %all-gather.9.cloned.1.call-update) | async-done | bytes 2097168 | tf_op jit(solution)/shard_map/all_gather | solution.py:91
  460.2 52.4 %while.20 = (s32[]{:T(128)}, f32[1,4,128,1]{2,1,3,0:T(4,128)S(1)}, f32[1,4,128,1]{2,1,3,0:T(4,128)S(1)}, f32[1,4,128,128]{3,2,1,0:T(8,128)S(1)}, s32[1,4]{1,0:T(...) while((s32[]{:T(128)}, f32[1,4,128,1]{2,1,3,0:T(4,128)S(1)}, ...), condition=%wide.region_7.8_spmd.clone, body=%wide.region_3.7_spmd.clone.sunk | while | flops 137050240 | bytes 4371203 | solution.py:130
  460.3 0.3 and_and_fusion.2
  460.6 1.2 fusion.50
  462.1 1.3 fusion.53
  463.6 0.3 and_and_fusion.2
  463.9 1.2 fusion.50
  465.4 1.3 fusion.53
  466.9 0.3 and_and_fusion.2
  467.2 1.2 fusion.50
  468.7 1.3 fusion.53
  470.2 0.3 and_and_fusion.2
  470.4 1.2 fusion.50
  472.0 1.3 fusion.53
  473.4 0.3 and_and_fusion.2
  473.7 1.2 fusion.50
  475.2 1.3 fusion.53
  476.7 0.3 and_and_fusion.2
  477.0 1.2 fusion.50
  478.5 1.3 fusion.53
  480.0 0.3 and_and_fusion.2
  480.3 1.2 fusion.50
  481.8 1.3 fusion.53
  483.3 0.3 and_and_fusion.2
  483.6 1.2 fusion.50
  485.1 1.3 fusion.53
  486.6 0.3 and_and_fusion.2
  486.8 1.2 fusion.50
  488.3 1.3 fusion.53
  489.8 0.3 and_and_fusion.2
  490.1 1.2 fusion.50
  491.6 1.3 fusion.53
  493.1 0.3 and_and_fusion.2
  493.4 1.2 fusion.50
  494.9 1.3 fusion.53
  496.4 0.3 and_and_fusion.2
  496.7 1.2 fusion.50
  498.2 1.3 fusion.53
  499.7 0.3 and_and_fusion.2
  499.9 1.2 fusion.50
  501.4 1.3 fusion.53
  502.9 0.3 and_and_fusion.2
  503.2 1.2 fusion.50
  504.7 1.3 fusion.53
  506.2 0.3 and_and_fusion.2
  506.5 1.2 fusion.50
  508.0 1.3 fusion.53
  509.5 0.3 and_and_fusion.2
  509.8 1.2 fusion.50
  511.3 1.3 fusion.53
  512.9 0.7 copy.49
  (171 shorter events, 6.9 us)
Async XLA Ops:
  7.2 27.9 %copy-start.1 = (bf16[7168]{0:T(1024)(128)(2,1)S(1)}, bf16[7168]{0:T(1024)(128)(2,1)}, u32[]{:S(2)}) copy-start(bf16[7168]{0:T(1024)(128)(2,1)} %param.9) | copy-start | bytes 43012
  7.2 27.9 %copy-start.2 = (s32[4]{0:T(128)S(1)}, s32[4]{0:T(128)}, u32[]{:S(2)}) copy-start(s32[4]{0:T(128)} %param.13) | copy-start | bytes 52
  7.2 28.2 %copy-start = (bf16[128,7168]{1,0:T(8,128)(2,1)S(1)}, bf16[128,7168]{1,0:T(8,128)(2,1)}, u32[]{:S(2)}) copy-start(bf16[128,7168]{1,0:T(8,128)(2,1)} %param.8) | copy-start | bytes 5505028
  7.2 223.9 %all-gather.5.cloned.1.call-start = ((), (), s32[]{:S(2)}) async-start(), calls=%async_computation.1 | async-start | bytes 11182080 | tf_op jit(solution)/shard_map/all_gather | solution.py:62
  35.0 313.2 %all-gather.7.cloned.1.call-start = ((), (), s32[]{:S(2)}) async-start(), calls=%async_computation.2 | async-start | bytes 2129920 | tf_op jit(solution)/shard_map/all_gather | solution.py:90
  239.1 221.1 %all-gather.9.cloned.1.call-start = ((), (), s32[]{:S(2)}) async-start(), calls=%async_computation.3 | async-start | bytes 2129920 | tf_op jit(solution)/shard_map/all_gather | solution.py:91
Sparse Core Ops, SparseCore 0:
  35.1 195.9 all-gather.4
  239.3 108.8 all-gather.6
  352.4 107.7 all-gather.8
where the time goes:
time: 521 us; the launch traced here: 520 us
  waiting for transfers between devices  413 us (79%)
  matrix products  48.6 us (9%)
  blocking collectives  24 us (5%)
  other arithmetic  14.5 us (3%)
  between operations  14 us (3%)
    all_gather x1, waiting for transfers between devices, per_device(): lax.all_gather(serving_combined, 'dp', axis=0, tiled=True)  195 us
    all_gather x1, waiting for transfers between devices, per_device(): value_piece = lax.all_gather(content_vectors, 'dp', axis=0, tiled=True)  112 us
    all_gather x1, waiting for transfers between devices, per_device(): key_piece = lax.all_gather(spun_lookup_vectors, 'dp', axis=0, tiled=True)  106 us
    all_to_all x1, blocking collectives, per_device(): lax.all_to_all(combined_slab, 'tensor', split_axis=1, concat_axis=0, tile...  24 us
    dot_general x16, matrix products, one_step(): jnp.einsum('ghqk,kgd->ghqd', weights.astype(jnp.bfloat16), values_three,...  21.5 us
    dot_general x16, matrix products, one_step(): jnp.einsum('ghqd,kgd->ghqk', probe_vectors, keys_three, preferred_element...  19.9 us
  transfers between devices with their start and end apart: 3, of which 3 were waited for; matrix products, arithmetic and copies ran while one was open for 1% of the time, Pallas kernels for 0%

commit v1 on v0

--- a/solution.py
+++ b/solution.py
@@ -10,6 +10,12 @@
 rope_theta = 5000000.0
 norm_eps = 1e-05
 masked_score = -1e30
+
+
+def recover_series(own_rows):
+    back = jnp.stack([own_rows for _ in range(jax.lax.axis_size("dp"))], axis=0)
+    opened = jax.lax.all_to_all(back, axis_name="dp", split_axis=0, concat_axis=0)
+    return jnp.concatenate(opened, axis=0)
 
 
 def document_start(lengths, positions):
@@ -58,9 +64,7 @@
     scale = lax.rsqrt(jnp.mean(widened * widened, axis=1, keepdims=True) + norm_eps)
     normed = (widened * scale * norm_gain.astype(jnp.float32)[None, :]).astype(jnp.bfloat16)
     mapped_result = jnp.dot(
-        normed,
-        lax.all_gather(serving_combined, "dp", axis=0, tiled=True),
-        preferred_element_type=jnp.float32,
+        normed, recover_series(serving_combined), preferred_element_type=jnp.float32
     )
     mapped_result = mapped_result.reshape(tok_rows, local_groups, QUARTET_SHARE + 2, PER_ATTN_DIM)
     query_part = mapped_result[:, :, :QUARTET_SHARE, :]

time: 521 us -> 885 us (1.70)
  waiting for transfers between devices: 413 us -> 741 us
  local copies, waits for them, and re-layouts: 4.69 us -> 23.5 us
  starting transfers between devices: 0.12 us -> 17.3 us
    all_gather x1, waiting for transfers between devices: 106 us -> 403 us  [per_device(): key_piece = lax.all_gather(spun_lookup_vectors, 'dp', axis=0, tiled=True)]
    all_to_all x0 -> x1, waiting for transfers between devices: none -> 226 us  [recover_series(): jax.lax.all_to_all(back, axis_name='dp', split_axis=0, concat_axis=0)]
    all_gather x1 -> x0, waiting for transfers between devices: 195 us -> none  [per_device(): lax.all_gather(serving_combined, 'dp', axis=0, tiled=True)]
    all_to_all x0 -> x1, starting transfers between devices: none -> 17.3 us  [recover_series(): jax.lax.all_to_all(back, axis_name='dp', split_axis=0, concat_axis=0)]
    dot_general x0 -> x1, local copies, waits for them, and re-layouts: none -> 14.7 us  [per_device(): jnp.dot(normed, recover_series(serving_combined), preferred_element_type=...]
  transfers between devices with their start and end apart: 3 -> 3, of which waited for: 3 -> 3; matrix products, arithmetic and copies ran while one was open for 1% -> 0% of each run, Pallas kernels for 0% -> 0%
where the time goes in v1:
time: 885 us; the launch traced here: 883 us
  waiting for transfers between devices  741 us (84%)
  matrix products  47.4 us (5%)
  blocking collectives  24 us (3%)
  local copies, waits for them, and re-layouts  23.5 us (3%)
  starting transfers between devices  17.3 us (2%)
  other arithmetic  14.3 us (2%)
  between operations  14.3 us (2%)
    all_gather x1, waiting for transfers between devices, per_device(): key_piece = lax.all_gather(spun_lookup_vectors, 'dp', axis=0, tiled=True)  403 us
    all_to_all x1, waiting for transfers between devices, recover_series(): jax.lax.all_to_all(back, axis_name='dp', split_axis=0, concat_axis=0)  226 us
    all_gather x1, waiting for transfers between devices, per_device(): value_piece = lax.all_gather(content_vectors, 'dp', axis=0, tiled=True)  112 us
    all_to_all x1, blocking collectives, per_device(): lax.all_to_all(combined_slab, 'tensor', split_axis=1, concat_axis=0, tile...  24 us
    dot_general x16, matrix products, one_step(): jnp.einsum('ghqk,kgd->ghqd', weights.astype(jnp.bfloat16), values_three,...  21.5 us
    dot_general x16, matrix products, one_step(): jnp.einsum('ghqd,kgd->ghqk', probe_vectors, keys_three, preferred_element...  19.9 us
  transfers between devices with their start and end apart: 3, of which 3 were waited for; matrix products, arithmetic and copies ran while one was open for 0% of the time, Pallas kernels for 0%

profile of v1, /device:TPU:1, one launch (start us, length us, event | category | flops | bytes accessed | tf_op | source)
XLA Modules:
  0.0 883.2 jit_solution(736384294019914806)
XLA Ops:
  7.2 0.8 convert.33
  8.1 0.8 convert.32
  8.9 1.0 convert.31
  10.0 24.0 %all_to_all.21 = bf16[14,8,768]{2,0,1:T(8,128)(2,1)S(1)} all-to-all(bf16[14,8,768]{2,0,1:T(8,128)(2,1)S(1)} %pad_maximum_fusion), channel_id=1, replica_groups=mesh['dp'=64,'tensor'=8] {'tensor'}, dimensions={1} | all-to-all | bytes 344064 | tf_op jit(solution)/shard_map/all_to_all | solution.py:59
  34.1 4.7 stack.2
  38.9 17.3 %all-to-all-start.1 = ((bf16[64,112,768]{2,1,0:T(8,128)(2,1)}), bf16[64,112,768]{2,1,0:T(8,128)(2,1)}, u32[]{:S(2)}, u32[]{:S(2)}) async-start(bf16[64,112,768]{2,1,0:T(8,128)(2,1)} %stack.2), calls=%async_computation.1 | async-start | bytes 22020096 | tf_op jit(solution)/shard_map/all_to_all | solution.py:17
  56.5 0.4 fusion.20
  57.0 226.2 %all-to-all-done.1 = bf16[64,112,768]{2,1,0:T(8,128)(2,1)} async-done(((bf16[64,112,768]{2,1,0:T(8,128)(2,1)}), bf16[64,112,768]{2,1,0:T(8,128)(2,1)}, u32[]{:S(2)}, u32[]{:S(2)}) %all-to-all-start.1) | async-done | bytes 11010080 | tf_op jit(solution)/shard_map/all_to_all | solution.py:17
  283.2 14.7 %copy.36 = bf16[768,7168]{1,0:T(8,128)(2,1)} copy(bf16[768,7168]{0,1:T(8,128)(2,1)} %bitcast.3) | data formatting | bytes 22020096 | tf_op jit(solution)/shard_map/dot_general | solution.py:66
  297.9 5.9 fusion.28
  304.0 0.6 pad_maximum_fusion.1
  304.7 0.6 slice.66
  305.6 1.5 copy.41
  307.1 0.7 copy.42
  308.1 403.0 %all-gather.4.cloned.1.call-done = bf16[8192,128]{0,1:T(8,128)(2,1)} async-done(((bf16[128,128]{0,1:T(8,128)(2,1)}), bf16[8192,128]{0,1:T(8,128)(2,1)}) %all-gather.4.cloned.1.call-update) | async-done | bytes 2097168 | tf_op jit(solution)/shard_map/all_gather | solution.py:94
  711.0 112.0 %all-gather.6.cloned.1.call-done = bf16[8192,1,1,128]{0,3,2,1:T(8,128)(2,1)} async-done(((bf16[128,1,1,128]{0,3,2,1:T(8,128)(2,1)}), bf16[8192,1,1,128]{0,3,2,1:T(8,128)(2,1)}) %all-gather.6.cloned.1.call-update) | async-done | bytes 2097168 | tf_op jit(solution)/shard_map/all_gather | solution.py:95
  823.1 52.4 %while.20 = (s32[]{:T(128)}, f32[1,4,128,1]{2,1,3,0:T(4,128)S(1)}, f32[1,4,128,1]{2,1,3,0:T(4,128)S(1)}, f32[1,4,128,128]{3,2,1,0:T(8,128)S(1)}, s32[1,4]{1,0:T(...) while((s32[]{:T(128)}, f32[1,4,128,1]{2,1,3,0:T(4,128)S(1)}, ...), condition=%wide.region_7.8_spmd.clone, body=%wide.region_3.7_spmd.clone.sunk | while | flops 137050240 | bytes 4371203 | solution.py:134
  823.2 0.3 and_and_fusion.2
  823.4 1.2 fusion.54
  824.9 1.3 fusion.57
  826.4 0.3 and_and_fusion.2
  826.7 1.2 fusion.54
  828.2 1.3 fusion.57
  829.7 0.3 and_and_fusion.2
  830.0 1.2 fusion.54
  831.5 1.3 fusion.57
  833.0 0.3 and_and_fusion.2
  833.3 1.2 fusion.54
  834.8 1.3 fusion.57
  836.3 0.3 and_and_fusion.2
  836.5 1.2 fusion.54
  838.1 1.3 fusion.57
  839.5 0.3 and_and_fusion.2
  839.8 1.2 fusion.54
  841.3 1.3 fusion.57
  842.8 0.3 and_and_fusion.2
  843.1 1.2 fusion.54
  844.6 1.3 fusion.57
  846.1 0.3 and_and_fusion.2
  846.4 1.2 fusion.54
  847.9 1.3 fusion.57
  849.4 0.3 and_and_fusion.2
  849.7 1.2 fusion.54
  851.2 1.3 fusion.57
  852.7 0.3 and_and_fusion.2
  852.9 1.2 fusion.54
  854.4 1.3 fusion.57
  855.9 0.3 and_and_fusion.2
  856.2 1.2 fusion.54
  857.7 1.3 fusion.57
  859.2 0.3 and_and_fusion.2
  859.5 1.2 fusion.54
  861.0 1.3 fusion.57
  862.5 0.3 and_and_fusion.2
  862.8 1.2 fusion.54
  864.3 1.3 fusion.57
  865.8 0.3 and_and_fusion.2
  866.0 1.2 fusion.54
  867.6 1.3 fusion.57
  869.3 1.2 fusion.54
  870.8 1.3 fusion.57
  872.6 1.2 fusion.54
  874.1 1.3 fusion.57
  875.7 0.7 copy.51
  (174 shorter events, 7.5 us)
Async XLA Ops:
  34.1 4.8 copy-start.1
  38.9 17.3 %copy-start.2 = (bf16[7168]{0:T(1024)(128)(2,1)S(1)}, bf16[7168]{0:T(1024)(128)(2,1)}, u32[]{:S(2)}) copy-start(bf16[7168]{0:T(1024)(128)(2,1)} %param.9) | copy-start | bytes 43012
  38.9 17.4 %copy-start.3 = (s32[4]{0:T(128)S(1)}, s32[4]{0:T(128)}, u32[]{:S(2)}) copy-start(s32[4]{0:T(128)} %param.13) | copy-start | bytes 52
  38.9 17.7 %copy-start = (bf16[128,7168]{1,0:T(8,128)(2,1)S(1)}, bf16[128,7168]{1,0:T(8,128)(2,1)}, u32[]{:S(2)}) copy-start(bf16[128,7168]{1,0:T(8,128)(2,1)} %param.8) | copy-start | bytes 5505028
  38.9 244.3 %all-to-all-start.1 = ((bf16[64,112,768]{2,1,0:T(8,128)(2,1)}), bf16[64,112,768]{2,1,0:T(8,128)(2,1)}, u32[]{:S(2)}, u32[]{:S(2)}) async-start(bf16[64,112,768]{2,1,0:T(8,128)(2,1)} %stack.2), calls=%async_computation.1 | async-start | bytes 22020096 | tf_op jit(solution)/shard_map/all_to_all | solution.py:17
  56.1 654.9 %all-gather.4.cloned.1.call-start = ((), (), s32[]{:S(2)}) async-start(), calls=%async_computation.2 | async-start | bytes 2129920 | tf_op jit(solution)/shard_map/all_gather | solution.py:94
  304.7 518.4 %all-gather.6.cloned.1.call-start = ((), (), s32[]{:S(2)}) async-start(), calls=%async_computation.3 | async-start | bytes 2129920 | tf_op jit(solution)/shard_map/all_gather | solution.py:95
Sparse Core Ops, SparseCore 0:
  304.8 406.2 all-gather.3
  715.2 107.7 all-gather.5
